TPU v7x, 32 devices: a whole 2x2x4 slice. The times are simulated.
32 devices in a mesh: group: 4 (over y, x), member: 8 (over z, core).
Axes of the slice: x: 2, y: 2, z: 4, core: 2. Of those that a mesh axis runs over, the one named last changes fastest.
Arguments:
- picture_embedding_matrix: bfloat16 [8192, 1152], P(('group', 'member')), may hold values from -1 to 1
- caption_embedding_matrix: bfloat16 [8192, 1152], P(('group', 'member')), may hold values from -1 to 1
- learned_sharpness: float32 [1], replicated, may hold values from 5 to 20
- learned_offset_entry: float32 [1], replicated, may hold values from -4 to -2
Outputs:
- grad_images: float32 [8192, 1152], P(('group', 'member'))
- grad_texts: float32 [8192, 1152], P(('group', 'member'))
All inputs are finite; a program needn't handle non-finite values.
Results may differ from a plain program's by a relative error of at most 0.002.
Values may be sent and summed in bfloat16 or wider, within the bound.
A program may use at most 192 MiB of HBM per device.

v0:
```python
import functools

import jax
import jax.numpy as jnp
from jax import lax
from jax.experimental import pallas as pl
from jax.experimental.pallas import tpu as pltpu
from jax.sharding import PartitionSpec as P

MESH = pl.DeviceIdType.MESH
F32 = jnp.float32
PIECES = 4
SKEW = 2
EARLY = 2


def contract(a, b, da, db):
    return lax.dot_general(a, b, (((da,), (db,)), ((), ())), preferred_element_type=F32)


def kernel(
    groups, n, sharp_ref, bias_ref, img_ref, txt_ref, gi_ref, gt_ref,
    other, gi_other, gi_in, txt_prev, img_next, tbuf, coef, gin, gout, vin, vout,
    t_send, t_recv, g_send, g_recv, v_send, v_recv, x_send, x_recv,
):
    rows, width = img_ref.shape
    piece = rows // PIECES
    group = lax.axis_index("group")
    member = lax.axis_index("member")
    chip, core = member // 2, member % 2
    partner = (group, member + 1 - 2 * core)
    ahead = ((group + 1) % groups, member)
    behind = ((group + groups - 1) % groups, member)
    right, left = (group, member + 2), (group, member - 2)
    has_right, has_left = chip + 1 < n, chip > 0
    sharp, bias = sharp_ref[0], bias_ref[0]

    barrier = pltpu.get_barrier_semaphore()
    for device in (partner, ahead, behind):
        pl.semaphore_signal(barrier, inc=1, device_id=device, device_id_type=MESH)
    for exists, device in ((has_right, right), (has_left, left)):
        @pl.when(exists)
        def _():
            pl.semaphore_signal(barrier, inc=1, device_id=device, device_id_type=MESH)
    pl.semaphore_wait(barrier, 3 + has_right.astype(jnp.int32) + has_left.astype(jnp.int32))

    def remote(src, dst, send, recv, device):
        return pltpu.make_async_remote_copy(
            src_ref=src, dst_ref=dst, send_sem=send, recv_sem=recv,
            device_id=device, device_id_type=MESH,
        )

    def part_of(p):
        return pl.ds(pl.multiple_of(p * piece, piece), piece)

    def own_text(slot, p, device):
        return remote(
            txt_ref.at[part_of(p)], tbuf.at[chip, part_of(p)],
            t_send.at[slot, p], t_recv.at[chip, p], device,
        )

    def passed_text(b, p, device):
        block = tbuf.at[b, part_of(p)]
        return remote(block, block, t_send.at[b, p], t_recv.at[b, p], device)

    def sums(b, slot, p, device):
        return remote(gout.at[b, p], gin.at[slot, p], g_send.at[b, p], g_recv.at[slot, p], device)

    def means(b, slot, p, device):
        return remote(vout.at[b, p], vin.at[slot, p], v_send.at[b, p], v_recv.at[slot, p], device)

    swap = remote(img_ref, other, x_send.at[0], x_recv.at[0], partner)
    to_ahead = remote(txt_ref, txt_prev, x_send.at[1], x_recv.at[1], ahead)
    to_behind = remote(img_ref, img_next, x_send.at[2], x_recv.at[2], behind)
    give = remote(gi_other, gi_in, x_send.at[3], x_recv.at[3], partner)

    swap.start()

    for p in range(PIECES):
        @pl.when(has_right)
        def _():
            own_text(chip, p, right).start()

        @pl.when(has_left)
        def _():
            own_text(n, p, left).start()

    to_ahead.start()
    to_behind.start()

    def weights(dots, matching):
        logits = sharp * dots + bias
        if matching:
            hit = lax.broadcasted_iota(jnp.int32, dots.shape, 0) == lax.broadcasted_iota(
                jnp.int32, dots.shape, 1
            )
            sign = jnp.where(hit, 1.0, -1.0).astype(F32)
            return (-sign * (sharp / (1.0 + jnp.exp(sign * logits)))).astype(jnp.bfloat16)
        return (sharp / (1.0 + jnp.exp(-logits))).astype(jnp.bfloat16)

    def weigh(b, part):
        for half, img in ((0, img_ref), (1, other)):
            coef[b, half, part, :] = weights(contract(tbuf[b, part, :], img[...], 1, 1), False)

    def add_images(b):
        for half, total in ((0, gi_ref), (1, gi_other)):
            total[...] += contract(coef[b, half], tbuf[b], 0, 0)

    def share(b, p):
        part = part_of(p)
        return contract(coef[b, 0, part, :], img_ref[...], 1, 0) + contract(
            coef[b, 1, part, :], other[...], 1, 0
        )

    c = weights(contract(txt_ref[...], img_ref[...], 1, 1), True)
    gi_ref[...] = contract(c, txt_ref[...], 0, 0)
    gt_ref[...] = contract(c, img_ref[...], 1, 0)
    swap.wait()
    c = weights(contract(txt_ref[...], other[...], 1, 1), False)
    gi_other[...] = contract(c, txt_ref[...], 0, 0)
    gt_ref[...] += contract(c, other[...], 1, 0)

    def send_on(b, slot, p, total, mean, device):
        middle = jnp.mean(total, axis=0, keepdims=True)
        gout[b, p] = (total - middle).astype(jnp.bfloat16)
        vout[b, p] = middle if mean is None else middle + mean
        sums(b, slot, p, device).start()
        means(b, slot, p, device).start()

    def arrived(slot, p):
        sums(0, slot, p, partner).wait_recv()
        means(0, slot, p, partner).wait_recv()

    def slot_right(b):
        return jnp.where(chip + 1 == b, n, b)

    def phase(t, carry):
        from_left, from_right = chip - t, chip + t
        low, high = n - 1 - t, t
        sides = (
            (from_left >= 0, from_left, has_right, right, left, from_left),
            (from_right < n, from_right, has_left, left, right, slot_right(from_right)),
        )

        @pl.loop(0, PIECES)
        def _(p):
            for valid, b, more, onward, back, slot in sides:
                @pl.when(valid)
                def _():
                    passed_text(b, p, partner).wait_recv()

                    @pl.when(more)
                    def _():
                        passed_text(b, p, onward).start()

                    @pl.when(jnp.logical_not(more))
                    def _():
                        weigh(b, part_of(p))

                        @pl.when((t > 1) | (p < EARLY))
                        def _():
                            send_on(b, slot, p, share(b, p), None, back)

        for more, b, slot, back in (
            (has_right, chip - 1, chip - 1, left),
            (has_left, chip + 1, n, right),
        ):
            @pl.when((t == n - 1) & jnp.logical_not(more))
            def _():
                @pl.loop(EARLY, PIECES)
                def _(p):
                    send_on(b, slot, p, share(b, p), None, back)

        for valid, b, more, onward, back, slot in sides:
            @pl.when(valid)
            def _():
                @pl.when(more)
                def _():
                    weigh(b, pl.ds(0, rows))

                add_images(b)

        @pl.when(t == n - 1)
        def _():
            give.start()

        @pl.when(has_left & has_right & ((low < chip) | (high > chip)))
        def _():
            @pl.loop(0, PIECES + SKEW * (n - 1))
            def _(step):
                p_low, p_high = step - SKEW * (n - 1 - chip), step - SKEW * chip

                @pl.when((low < chip) & (p_low >= 0) & (p_low < PIECES))
                def _():
                    here = share(low, p_low)
                    arrived(low, p_low)
                    total = here + gin[low, p_low].astype(F32)
                    send_on(low, low, p_low, total, vin[low, p_low], left)

                @pl.when((high > chip) & (p_high >= 0) & (p_high < PIECES))
                def _():
                    here = share(high, p_high)
                    arrived(high, p_high)
                    total = here + gin[high, p_high].astype(F32)
                    send_on(high, slot_right(high), p_high, total, vin[high, p_high], right)

        return carry

    lax.fori_loop(1, n, phase, 0)

    to_ahead.wait_recv()
    c = weights(contract(img_ref[...], txt_prev[...], 1, 1), False)
    gi_ref[...] += contract(c, txt_prev[...], 1, 0)
    to_behind.wait_recv()
    c = weights(contract(txt_ref[...], img_next[...], 1, 1), False)
    gt_ref[...] += contract(c, img_next[...], 1, 0)
    give.wait_recv()
    gi_ref[...] += gi_in[...]

    for exists, slot in ((has_left, n), (has_right, chip)):
        @pl.when(exists)
        def _():
            @pl.loop(0, PIECES)
            def _(p):
                arrived(slot, p)
                gt_ref[part_of(p), :] += gin[slot, p].astype(F32) + vin[slot, p]

    give.wait_send()
    to_ahead.wait_send()
    to_behind.wait_send()

    @pl.loop(0, PIECES)
    def _(p):
        @pl.when(has_right)
        def _():
            own_text(chip, p, right).wait_send()

        @pl.when(has_left)
        def _():
            own_text(n, p, left).wait_send()

        @pl.loop(0, n)
        def _(b):
            @pl.when(((b < chip) & has_right) | ((b > chip) & has_left))
            def _():
                passed_text(b, p, partner).wait_send()

            @pl.when(b != chip)
            def _():
                sums(b, b, p, partner).wait_send()
                means(b, b, p, partner).wait_send()


def solution(mesh):
    groups, members = mesh.shape["group"], mesh.shape["member"]
    n = members // 2

    def shards(images, texts, sharpness, offset):
        rows, width = images.shape
        piece = rows // PIECES
        bf16 = jnp.bfloat16
        out = jax.ShapeDtypeStruct((rows, width), F32)
        vmem = pl.BlockSpec(memory_space=pltpu.VMEM)
        smem = pl.BlockSpec(memory_space=pltpu.SMEM)
        dma = pltpu.SemaphoreType.DMA
        return pl.pallas_call(
            functools.partial(kernel, groups, n),
            out_shape=(out, out),
            in_specs=[smem, smem, vmem, vmem],
            out_specs=(vmem, vmem),
            scratch_shapes=[
                pltpu.VMEM((rows, width), bf16),
                pltpu.VMEM((rows, width), F32),
                pltpu.VMEM((rows, width), F32),
                pltpu.VMEM((rows, width), bf16),
                pltpu.VMEM((rows, width), bf16),
                pltpu.VMEM((n, rows, width), bf16),
                pltpu.VMEM((n, 2, rows, rows), bf16),
                pltpu.VMEM((n + 1, PIECES, piece, width), bf16),
                pltpu.VMEM((n, PIECES, piece, width), bf16),
                pltpu.VMEM((n + 1, PIECES, 1, width), F32),
                pltpu.VMEM((n, PIECES, 1, width), F32),
                dma((n + 1, PIECES)),
                dma((n, PIECES)),
                dma((n, PIECES)),
                dma((n + 1, PIECES)),
                dma((n, PIECES)),
                dma((n + 1, PIECES)),
                dma((4,)),
                dma((4,)),
            ],
            compiler_params=pltpu.CompilerParams(
                collective_id=0, has_side_effects=True, vmem_limit_bytes=min(60, 16 + 3 * n) * 1024 * 1024
            ),
        )(sharpness, offset, images, texts)

    spec = P(("group", "member"), None)
    return jax.shard_map(
        shards, mesh=mesh, in_specs=(spec, spec, P(), P()), out_specs=(spec, spec), check_vma=False
    )
```

profile of v0, /device:TPU:0, one launch (start us, length us, event | category | flops | bytes accessed | tf_op | source)
XLA Modules:
  0.0 72.3 jit_solution(7625207139613978939)
XLA Ops:
  1.9 0.0 copy-start
  1.9 1.1 %copy-done = bf16[256,1152]{1,0:T(8,128)(2,1)S(1)} copy-done((bf16[256,1152]{1,0:T(8,128)(2,1)S(1)}, bf16[256,1152]{1,0:T(8,128)(2,1)}, u32[]{:S(2)}) %copy-start) | copy-done | bytes 589848
  3.0 0.0 copy-start.1
  3.0 1.1 %copy-done.1 = bf16[256,1152]{1,0:T(8,128)(2,1)S(1)} copy-done((bf16[256,1152]{1,0:T(8,128)(2,1)S(1)}, bf16[256,1152]{1,0:T(8,128)(2,1)}, u32[]{:S(2)}) %copy-start.1) | copy-done | bytes 589848
  4.1 66.2 %shard_map.59 = (f32[256,1152]{1,0:T(8,128)S(1)}, f32[256,1152]{1,0:T(8,128)S(1)}) custom-call(f32[1]{0:T(128)S(6)} %copy.8.sharp_ref, f32[1]{0:T(128)S(6)} %copy.9.bias_ref, bf16[256,1152]{1,0:T(8,128)(2,1)S(1)} %copy-done, bf16[256,1152]{1,0:T(8,128)(2,1)S(1)} %copy-done.1), custom_call_target="tpu_custom_call" | custom-call | tf_op jit(solution)/shard_map/pallas_call | solution.py:266
  70.2 1.0 %copy.10 = f32[256,1152]{1,0:T(8,128)} copy(f32[256,1152]{1,0:T(8,128)S(1)} %get-tuple-element.4) | data formatting | bytes 2359296
  71.3 1.0 %copy.11 = f32[256,1152]{1,0:T(8,128)} copy(f32[256,1152]{1,0:T(8,128)S(1)} %get-tuple-element.5) | data formatting | bytes 2359296
Async XLA Ops:
  1.9 1.1 %copy-start = (bf16[256,1152]{1,0:T(8,128)(2,1)S(1)}, bf16[256,1152]{1,0:T(8,128)(2,1)}, u32[]{:S(2)}) copy-start(bf16[256,1152]{1,0:T(8,128)(2,1)} %img_ref.1) | copy-start | bytes 1769476
  3.0 1.1 %copy-start.1 = (bf16[256,1152]{1,0:T(8,128)(2,1)S(1)}, bf16[256,1152]{1,0:T(8,128)(2,1)}, u32[]{:S(2)}) copy-start(bf16[256,1152]{1,0:T(8,128)(2,1)} %txt_ref.1) | copy-start | bytes 1769476
where the time goes:
time: 72.5 us; the launch traced here: 72.3 us
  Pallas kernels  66.2 us (91%)
  local copies, waits for them, and re-layouts  4.15 us (6%)
  between operations  1.94 us (3%)
    pallas_call x1, Pallas kernels, shards(): pl.pallas_call(functools.partial(kernel, groups, n), out_shape=(out, out)...  66.2 us
    unnamed x6, local copies, waits for them, and re-layouts  4.15 us

commit v1 on v0

v1 whole, which is shorter than its diff:
```python
import functools

import jax
import jax.numpy as jnp
from jax import lax
from jax.experimental import pallas as pl
from jax.experimental.pallas import tpu as pltpu
from jax.sharding import PartitionSpec as P

MESH = pl.DeviceIdType.MESH
F32 = jnp.float32
PIECES = 8
HOP = 4
AHEAD = 2
LAG = 1


def contract(a, b, da, db):
    return lax.dot_general(a, b, (((da,), (db,)), ((), ())), preferred_element_type=F32)


def order(i, k, n):
    own = jnp.minimum(HOP * k, PIECES)
    j = i - own
    far = (j >= 0) & (j < k * PIECES)
    text_b = jnp.where(far, j // PIECES, k)
    text_p = jnp.where(far, j % PIECES, jnp.where(j < 0, i, i - k * PIECES))
    near = jnp.where(k == 0, HOP, 0)
    i = i - (k + 1) * PIECES
    j, rest = i - near, (n - 2 - k) * PIECES
    far = (j >= 0) & (j < rest)
    sum_b = jnp.where(far, n - 1 - j // PIECES, k + 1)
    sum_p = jnp.where(far, j % PIECES, jnp.where(j < 0, i, i - rest))
    is_text = i < 0
    return is_text, jnp.where(is_text, text_b, sum_b), jnp.where(is_text, text_p, sum_p)


def kernel(
    groups, n, sharp_ref, bias_ref, img_hbm, txt_hbm, gi_ref, gt_ref,
    img_ref, other, gi_other, gi_in, txt_prev, img_next, tbuf, coef, gin, gout, vin, vout,
    t_send, t_recv, g_send, g_recv, v_send, v_recv, x_send, x_recv, l_sem,
):
    rows, width = img_ref.shape
    piece = rows // PIECES
    group = lax.axis_index("group")
    member = lax.axis_index("member")
    chip, core = member // 2, member % 2
    partner = (group, member + 1 - 2 * core)
    ahead = ((group + 1) % groups, member)
    behind = ((group + groups - 1) % groups, member)
    right, left = (group, member + 2), (group, member - 2)
    has_right, has_left = chip + 1 < n, chip > 0
    sharp, bias = sharp_ref[0], bias_ref[0]

    load_txt = pltpu.make_async_copy(txt_hbm, tbuf.at[chip], l_sem.at[0])
    load_img = pltpu.make_async_copy(img_hbm, img_ref, l_sem.at[1])
    load_txt.start()
    load_img.start()

    barrier = pltpu.get_barrier_semaphore()
    for device in (partner, ahead, behind):
        pl.semaphore_signal(barrier, inc=1, device_id=device, device_id_type=MESH)
    for exists, device in ((has_right, right), (has_left, left)):
        @pl.when(exists)
        def _():
            pl.semaphore_signal(barrier, inc=1, device_id=device, device_id_type=MESH)
    pl.semaphore_wait(barrier, 3 + has_right.astype(jnp.int32) + has_left.astype(jnp.int32))

    def remote(src, dst, send, recv, device):
        return pltpu.make_async_remote_copy(
            src_ref=src, dst_ref=dst, send_sem=send, recv_sem=recv,
            device_id=device, device_id_type=MESH,
        )

    def part_of(p):
        return pl.ds(pl.multiple_of(p * piece, piece), piece)

    def text(b, slot, p, device):
        block = tbuf.at[b, part_of(p)]
        return remote(block, block, t_send.at[slot, p], t_recv.at[b, p], device)

    def sums(b, slot, p, device):
        return remote(gout.at[b, p], gin.at[slot, p], g_send.at[b, p], g_recv.at[slot, p], device)

    def means(b, slot, p, device):
        return remote(vout.at[b, p], vin.at[slot, p], v_send.at[b, p], v_recv.at[slot, p], device)

    swap = remote(img_ref, other, x_send.at[0], x_recv.at[0], partner)
    to_ahead = remote(tbuf.at[chip], txt_prev, x_send.at[1], x_recv.at[1], ahead)
    to_behind = remote(img_ref, img_next, x_send.at[2], x_recv.at[2], behind)
    give = remote(gi_other, gi_in, x_send.at[3], x_recv.at[3], partner)

    sides = (
        (chip, has_right, right, chip, n),
        (n - 1 - chip, has_left, left, n, chip),
    )

    def seen(side, b):
        return b if side == 0 else n - 1 - b

    load_txt.wait()
    for k, more, onward, own_slot, _ in sides:
        @pl.when(more)
        def _():
            for p in range(HOP):
                text(chip, own_slot, p, onward).start()
    load_img.wait()
    swap.start()
    to_ahead.start()
    to_behind.start()

    def weights(dots, matching):
        logits = sharp * dots + bias
        if matching:
            hit = lax.broadcasted_iota(jnp.int32, dots.shape, 0) == lax.broadcasted_iota(
                jnp.int32, dots.shape, 1
            )
            sign = jnp.where(hit, 1.0, -1.0).astype(F32)
            return (-sign * (sharp / (1.0 + jnp.exp(sign * logits)))).astype(jnp.bfloat16)
        return (sharp / (1.0 + jnp.exp(-logits))).astype(jnp.bfloat16)

    def weigh(b, part):
        for half, img in ((0, img_ref), (1, other)):
            coef[b, half, part, :] = weights(contract(tbuf[b, part, :], img[...], 1, 1), False)

    def add_images(b):
        for half, total in ((0, gi_ref), (1, gi_other)):
            total[...] += contract(coef[b, half], tbuf[b], 0, 0)

    def share(b, p):
        part = part_of(p)
        return contract(coef[b, 0, part, :], img_ref[...], 1, 0) + contract(
            coef[b, 1, part, :], other[...], 1, 0
        )

    def send_on(b, slot, p, total, mean, device):
        middle = jnp.mean(total, axis=0, keepdims=True)
        gout[b, p] = (total - middle).astype(jnp.bfloat16)
        vout[b, p] = middle if mean is None else middle + mean
        sums(b, slot, p, device).start()
        means(b, slot, p, device).start()

    def arrived(slot, p):
        sums(0, slot, p, partner).wait_recv()
        means(0, slot, p, partner).wait_recv()

    own = tbuf.at[chip]
    c = weights(contract(own[...], img_ref[...], 1, 1), True)
    gi_ref[...] = contract(c, own[...], 0, 0)
    gt_ref[...] = contract(c, img_ref[...], 1, 0)
    swap.wait()
    c = weights(contract(own[...], other[...], 1, 1), False)
    gi_other[...] = contract(c, own[...], 0, 0)
    gt_ref[...] += contract(c, other[...], 1, 0)

    total_pieces = n * PIECES
    window_at = (n - 1) * PIECES - 1
    give_at = (n - 1) * PIECES + LAG
    take_at = total_pieces - 2

    @pl.loop(0, total_pieces + LAG)
    def _(s):
        for side, (k, more, onward, own_slot, home) in enumerate(sides):
            i, j = s + AHEAD, s - LAG
            out_text, out_b, out_p = order(i, k, n)
            in_text, in_b, in_p = order(j, k - 1, n)
            out_b, in_b = seen(side, out_b), seen(side, in_b)
            going = more & (i < total_pieces)
            coming = (k > 0) & (j >= 0)

            @pl.when(going & out_text & (out_b == chip) & (i >= HOP))
            def _():
                text(chip, own_slot, out_p, onward).start()

            b, p = jnp.where(more, out_b, in_b), jnp.where(more, out_p, in_p)

            @pl.when((going & out_text & (out_b != chip)) | (jnp.logical_not(more) & coming & in_text))
            def _():
                text(b, b, p, onward).wait_recv()

                @pl.when(more)
                def _():
                    text(b, b, p, onward).start()

                weigh(b, part_of(p))

                @pl.when(p == PIECES - 1)
                def _():
                    add_images(b)

            @pl.when(going & jnp.logical_not(out_text))
            def _():
                arrives_at = chip + 1 - 2 * side
                slot = jnp.where(out_b == arrives_at, n if side == 0 else out_b, out_b)
                here = share(out_b, out_p)

                @pl.when(k == 0)
                def _():
                    send_on(out_b, slot, out_p, here, None, onward)

                @pl.when(k > 0)
                def _():
                    arrived(out_b, out_p)
                    send_on(
                        out_b, slot, out_p, here + gin[out_b, out_p].astype(F32), vin[out_b, out_p], onward
                    )

            @pl.when(coming & jnp.logical_not(in_text) & (in_b == chip))
            def _():
                arrived(home, in_p)
                gt_ref[part_of(in_p), :] += gin[home, in_p].astype(F32) + vin[home, in_p]

        @pl.when(s == window_at)
        def _():
            to_ahead.wait_recv()
            c = weights(contract(img_ref[...], txt_prev[...], 1, 1), False)
            gi_ref[...] += contract(c, txt_prev[...], 1, 0)
            to_behind.wait_recv()
            c = weights(contract(own[...], img_next[...], 1, 1), False)
            gt_ref[...] += contract(c, img_next[...], 1, 0)

        @pl.when(s == give_at)
        def _():
            give.start()

        @pl.when(s == take_at)
        def _():
            give.wait_recv()
            gi_ref[...] += gi_in[...]

    give.wait_send()
    to_ahead.wait_send()
    to_behind.wait_send()

    @pl.loop(0, PIECES)
    def _(p):
        @pl.when(has_right)
        def _():
            text(chip, chip, p, right).wait_send()

        @pl.when(has_left)
        def _():
            text(chip, n, p, left).wait_send()

        @pl.loop(0, n)
        def _(b):
            @pl.when(((b < chip) & has_right) | ((b > chip) & has_left))
            def _():
                text(b, b, p, partner).wait_send()

            @pl.when(b != chip)
            def _():
                sums(b, b, p, partner).wait_send()
                means(b, b, p, partner).wait_send()


def solution(mesh):
    groups, members = mesh.shape["group"], mesh.shape["member"]
    n = members // 2

    def shards(images, texts, sharpness, offset):
        rows, width = images.shape
        piece = rows // PIECES
        bf16 = jnp.bfloat16
        out = jax.ShapeDtypeStruct((rows, width), F32)
        vmem = pl.BlockSpec(memory_space=pltpu.VMEM)
        smem = pl.BlockSpec(memory_space=pltpu.SMEM)
        hbm = pl.BlockSpec(memory_space=pltpu.HBM)
        dma = pltpu.SemaphoreType.DMA
        return pl.pallas_call(
            functools.partial(kernel, groups, n),
            out_shape=(out, out),
            in_specs=[smem, smem, hbm, hbm],
            out_specs=(vmem, vmem),
            scratch_shapes=[
                pltpu.VMEM((rows, width), bf16),
                pltpu.VMEM((rows, width), bf16),
                pltpu.VMEM((rows, width), F32),
                pltpu.VMEM((rows, width), F32),
                pltpu.VMEM((rows, width), bf16),
                pltpu.VMEM((rows, width), bf16),
                pltpu.VMEM((n, rows, width), bf16),
                pltpu.VMEM((n, 2, rows, rows), bf16),
                pltpu.VMEM((n + 1, PIECES, piece, width), bf16),
                pltpu.VMEM((n, PIECES, piece, width), bf16),
                pltpu.VMEM((n + 1, PIECES, 1, width), F32),
                pltpu.VMEM((n, PIECES, 1, width), F32),
                dma((n + 1, PIECES)),
                dma((n, PIECES)),
                dma((n, PIECES)),
                dma((n + 1, PIECES)),
                dma((n, PIECES)),
                dma((n + 1, PIECES)),
                dma((4,)),
                dma((4,)),
                dma((2,)),
            ],
            compiler_params=pltpu.CompilerParams(
                collective_id=0, has_side_effects=True, vmem_limit_bytes=min(60, 16 + 3 * n) * 1024 * 1024
            ),
        )(sharpness, offset, images, texts)

    spec = P(("group", "member"), None)
    return jax.shard_map(
        shards, mesh=mesh, in_specs=(spec, spec, P(), P()), out_specs=(spec, spec), check_vma=False
    )
```

time: 72.5 us -> 67.3 us (0.928)
  Pallas kernels: 66.2 us -> 61 us
    pallas_call x1, Pallas kernels: 66.2 us -> 61 us  [shards(): pl.pallas_call(functools.partial(kernel, groups, n), out_shape=(out, out)...]
where the time goes in v1:
time: 67.3 us; the launch traced here: 67.1 us
  Pallas kernels  61 us (91%)
  local copies, waits for them, and re-layouts  4.15 us (6%)
  between operations  1.94 us (3%)
    pallas_call x1, Pallas kernels, shards(): pl.pallas_call(functools.partial(kernel, groups, n), out_shape=(out, out)...  61 us
    unnamed x6, local copies, waits for them, and re-layouts  4.15 us

profile of v1, /device:TPU:0, one launch (start us, length us, event | category | flops | bytes accessed | tf_op | source)
XLA Modules:
  0.0 67.1 jit_solution(14459453626342397028)
XLA Ops:
  1.9 0.0 copy-start
  1.9 1.1 %copy-done = bf16[256,1152]{1,0:T(8,128)(2,1)S(1)} copy-done((bf16[256,1152]{1,0:T(8,128)(2,1)S(1)}, bf16[256,1152]{1,0:T(8,128)(2,1)}, u32[]{:S(2)}) %copy-start) | copy-done | bytes 589848
  3.0 0.0 copy-start.1
  3.0 1.1 %copy-done.1 = bf16[256,1152]{1,0:T(8,128)(2,1)S(1)} copy-done((bf16[256,1152]{1,0:T(8,128)(2,1)S(1)}, bf16[256,1152]{1,0:T(8,128)(2,1)}, u32[]{:S(2)}) %copy-start.1) | copy-done | bytes 589848
  4.1 61.0 %shard_map.59 = (f32[256,1152]{1,0:T(8,128)S(1)}, f32[256,1152]{1,0:T(8,128)S(1)}) custom-call(f32[1]{0:T(128)S(6)} %copy.8.sharp_ref, f32[1]{0:T(128)S(6)} %copy.9.bias_ref, bf16[256,1152]{1,0:T(8,128)(2,1)S(1)} %copy-done, bf16[256,1152]{1,0:T(8,128)(2,1)S(1)} %copy-done.1), custom_call_target="tpu_custom_call" | custom-call | tf_op jit(solution)/shard_map/pallas_call | solution.py:270
  65.0 1.0 %copy.10 = f32[256,1152]{1,0:T(8,128)} copy(f32[256,1152]{1,0:T(8,128)S(1)} %get-tuple-element.4) | data formatting | bytes 2359296
  66.1 1.0 %copy.11 = f32[256,1152]{1,0:T(8,128)} copy(f32[256,1152]{1,0:T(8,128)S(1)} %get-tuple-element.5) | data formatting | bytes 2359296
Async XLA Ops:
  1.9 1.1 %copy-start = (bf16[256,1152]{1,0:T(8,128)(2,1)S(1)}, bf16[256,1152]{1,0:T(8,128)(2,1)}, u32[]{:S(2)}) copy-start(bf16[256,1152]{1,0:T(8,128)(2,1)} %img_hbm.1) | copy-start | bytes 1769476
  3.0 1.1 %copy-start.1 = (bf16[256,1152]{1,0:T(8,128)(2,1)S(1)}, bf16[256,1152]{1,0:T(8,128)(2,1)}, u32[]{:S(2)}) copy-start(bf16[256,1152]{1,0:T(8,128)(2,1)} %txt_hbm.1) | copy-start | bytes 1769476

commit v2 on v1

--- a/solution.py
+++ b/solution.py
@@ -77,13 +77,13 @@
 
     def text(b, slot, p, device):
         block = tbuf.at[b, part_of(p)]
-        return remote(block, block, t_send.at[slot, p], t_recv.at[b, p], device)
+        return remote(block, block, t_send.at[slot], t_recv.at[b, p], device)
 
     def sums(b, slot, p, device):
-        return remote(gout.at[b, p], gin.at[slot, p], g_send.at[b, p], g_recv.at[slot, p], device)
+        return remote(gout.at[b, p], gin.at[slot, p], g_send.at[b], g_recv.at[slot, p], device)
 
     def means(b, slot, p, device):
-        return remote(vout.at[b, p], vin.at[slot, p], v_send.at[b, p], v_recv.at[slot, p], device)
+        return remote(vout.at[b, p], vin.at[slot, p], v_send.at[b], v_recv.at[slot, p], device)
 
     swap = remote(img_ref, other, x_send.at[0], x_recv.at[0], partner)
     to_ahead = remote(tbuf.at[chip], txt_prev, x_send.at[1], x_recv.at[1], ahead)
@@ -227,31 +227,41 @@
         def _():
             give.wait_recv()
             gi_ref[...] += gi_in[...]
-
-    give.wait_send()
-    to_ahead.wait_send()
-    to_behind.wait_send()
-
-    @pl.loop(0, PIECES)
-    def _(p):
-        @pl.when(has_right)
-        def _():
-            text(chip, chip, p, right).wait_send()
-
-        @pl.when(has_left)
-        def _():
-            text(chip, n, p, left).wait_send()
-
-        @pl.loop(0, n)
-        def _(b):
-            @pl.when(((b < chip) & has_right) | ((b > chip) & has_left))
-            def _():
-                text(b, b, p, partner).wait_send()
-
-            @pl.when(b != chip)
-            def _():
-                sums(b, b, p, partner).wait_send()
-                means(b, b, p, partner).wait_send()
+            give.wait_send()
+            to_ahead.wait_send()
+            to_behind.wait_send()
+
+            def all_text(b, slot):
+                remote(tbuf.at[b], tbuf.at[b], t_send.at[slot], t_recv.at[b, 0], partner).wait_send()
+
+            for _, more, _, own_slot, _ in sides:
+                @pl.when(more)
+                def _():
+                    all_text(chip, own_slot)
+
+            @pl.loop(0, n)
+            def _(b):
+                @pl.when(((b < chip) & has_right) | ((b > chip) & has_left))
+                def _():
+                    all_text(b, b)
+
+    @pl.loop(0, n)
+    def _(b):
+        @pl.when(b != chip)
+        def _():
+            remote(gout.at[b], gout.at[b], g_send.at[b], g_recv.at[b, 0], partner).wait_send()
+            remote(vout.at[b], vout.at[b], v_send.at[b], v_recv.at[b, 0], partner).wait_send()
+
+
+def write_out(gi_ref, gt_ref, gi_out, gt_out, sem):
+    copies = [
+        pltpu.make_async_copy(gi_ref, gi_out, sem.at[0]),
+        pltpu.make_async_copy(gt_ref, gt_out, sem.at[1]),
+    ]
+    for copy in copies:
+        copy.start()
+    for copy in copies:
+        copy.wait()
 
 
 def solution(mesh):
@@ -267,7 +277,7 @@
         smem = pl.BlockSpec(memory_space=pltpu.SMEM)
         hbm = pl.BlockSpec(memory_space=pltpu.HBM)
         dma = pltpu.SemaphoreType.DMA
-        return pl.pallas_call(
+        gi, gt = pl.pallas_call(
             functools.partial(kernel, groups, n),
             out_shape=(out, out),
             in_specs=[smem, smem, hbm, hbm],
@@ -285,11 +295,11 @@
                 pltpu.VMEM((n, PIECES, piece, width), bf16),
                 pltpu.VMEM((n + 1, PIECES, 1, width), F32),
                 pltpu.VMEM((n, PIECES, 1, width), F32),
+                dma((n + 1,)),
+                dma((n, PIECES)),
+                dma((n,)),
                 dma((n + 1, PIECES)),
-                dma((n, PIECES)),
-                dma((n, PIECES)),
-                dma((n + 1, PIECES)),
-                dma((n, PIECES)),
+                dma((n,)),
                 dma((n + 1, PIECES)),
                 dma((4,)),
                 dma((4,)),
@@ -298,7 +308,15 @@
             compiler_params=pltpu.CompilerParams(
                 collective_id=0, has_side_effects=True, vmem_limit_bytes=min(60, 16 + 3 * n) * 1024 * 1024
             ),
-        )(sharpness, offset, images, texts)
+        )(sharpness, offset, *(pltpu.with_memory_space_constraint(a, pltpu.HBM) for a in (images, texts)))
+        return pl.pallas_call(
+            write_out,
+            out_shape=(out, out),
+            in_specs=[vmem, vmem],
+            out_specs=(hbm, hbm),
+            scratch_shapes=[dma((2,))],
+            compiler_params=pltpu.CompilerParams(vmem_limit_bytes=8 * 1024 * 1024),
+        )(gi, gt)
 
     spec = P(("group", "member"), None)
     return jax.shard_map(

time: 67.3 us -> 63 us (0.936)
  local copies, waits for them, and re-layouts: 4.15 us -> 0 us
    unnamed x6 -> x0, local copies, waits for them, and re-layouts: 4.15 us -> none
    pallas_call x1, Pallas kernels: 61 us -> 59.5 us  [shards(): pl.pallas_call(functools.partial(kernel, groups, n), out_shape=(out, out)...]
    pallas_call x0 -> x1, Pallas kernels: none -> 1.42 us  [shards(): pl.pallas_call(write_out, out_shape=(out, out), in_specs=[vmem, vmem], ou...]
where the time goes in v2:
time: 63 us; the launch traced here: 62.8 us
  Pallas kernels  60.9 us (97%)
  between operations  1.93 us (3%)
    pallas_call x1, Pallas kernels, shards(): pl.pallas_call(functools.partial(kernel, groups, n), out_shape=(out, out)...  59.5 us
    pallas_call x1, Pallas kernels, shards(): pl.pallas_call(write_out, out_shape=(out, out), in_specs=[vmem, vmem], ou...  1.42 us

profile of v2, /device:TPU:0, one launch (start us, length us, event | category | flops | bytes accessed | tf_op | source)
XLA Modules:
  0.0 62.8 jit_solution(5979643104051162675)
XLA Ops:
  1.9 59.5 %shard_map.59 = (f32[256,1152]{1,0:T(8,128)S(1)}, f32[256,1152]{1,0:T(8,128)S(1)}) custom-call(f32[1]{0:T(128)S(6)} %copy.6.sharp_ref, f32[1]{0:T(128)S(6)} %copy.7.bias_ref, bf16[256,1152]{1,0:T(8,128)(2,1)} %img_hbm.1, bf16[256,1152]{1,0:T(8,128)(2,1)} %txt_hbm.1), custom_call_target="tpu_custom_call" | custom-call | tf_op jit(solution)/shard_map/pallas_call | solution.py:280
  61.4 1.4 %shard_map.60 = (f32[256,1152]{1,0:T(8,128)}, f32[256,1152]{1,0:T(8,128)}) custom-call(f32[256,1152]{1,0:T(8,128)S(1)} %get-tuple-element.4.gi_ref, f32[256,1152]{1,0:T(8,128)S(1)} %get-tuple-element.5.gt_ref), custom_call_target="tpu_custom_call" | custom-call | tf_op jit(solution)/shard_map/pallas_call | solution.py:312

commit v3 on v2

--- a/solution.py
+++ b/solution.py
@@ -10,6 +10,8 @@
 MESH = pl.DeviceIdType.MESH
 F32 = jnp.float32
 PIECES = 8
+TALL = 1
+WRITES = 4
 HOP = 4
 AHEAD = 2
 LAG = 1
@@ -50,7 +52,6 @@
     behind = ((group + groups - 1) % groups, member)
     right, left = (group, member + 2), (group, member - 2)
     has_right, has_left = chip + 1 < n, chip > 0
-    sharp, bias = sharp_ref[0], bias_ref[0]
 
     load_txt = pltpu.make_async_copy(txt_hbm, tbuf.at[chip], l_sem.at[0])
     load_img = pltpu.make_async_copy(img_hbm, img_ref, l_sem.at[1])
@@ -108,6 +109,7 @@
     swap.start()
     to_ahead.start()
     to_behind.start()
+    sharp, bias = sharp_ref[0], bias_ref[0]
 
     def weights(dots, matching):
         logits = sharp * dots + bias
@@ -127,8 +129,11 @@
         for half, total in ((0, gi_ref), (1, gi_other)):
             total[...] += contract(coef[b, half], tbuf[b], 0, 0)
 
-    def share(b, p):
-        part = part_of(p)
+    def tall_part_of(q):
+        return pl.ds(pl.multiple_of(q * TALL * piece, TALL * piece), TALL * piece)
+
+    def share(b, q):
+        part = tall_part_of(q)
         return contract(coef[b, 0, part, :], img_ref[...], 1, 0) + contract(
             coef[b, 1, part, :], other[...], 1, 0
         )
@@ -152,6 +157,10 @@
     c = weights(contract(own[...], other[...], 1, 1), False)
     gi_other[...] = contract(c, own[...], 0, 0)
     gt_ref[...] += contract(c, other[...], 1, 0)
+
+    def all_sums(b):
+        remote(gout.at[b], gout.at[b], g_send.at[b], g_recv.at[b, 0], partner).wait_send()
+        remote(vout.at[b], vout.at[b], v_send.at[b], v_recv.at[b, 0], partner).wait_send()
 
     total_pieces = n * PIECES
     window_at = (n - 1) * PIECES - 1
@@ -188,27 +197,27 @@
                 def _():
                     add_images(b)
 
-            @pl.when(going & jnp.logical_not(out_text))
+            @pl.when(going & jnp.logical_not(out_text) & (out_p % TALL == TALL - 1))
             def _():
+                q = out_p // TALL
                 arrives_at = chip + 1 - 2 * side
                 slot = jnp.where(out_b == arrives_at, n if side == 0 else out_b, out_b)
-                here = share(out_b, out_p)
+                here = share(out_b, q)
 
                 @pl.when(k == 0)
                 def _():
-                    send_on(out_b, slot, out_p, here, None, onward)
+                    send_on(out_b, slot, q, here, None, onward)
 
                 @pl.when(k > 0)
                 def _():
-                    arrived(out_b, out_p)
-                    send_on(
-                        out_b, slot, out_p, here + gin[out_b, out_p].astype(F32), vin[out_b, out_p], onward
-                    )
-
-            @pl.when(coming & jnp.logical_not(in_text) & (in_b == chip))
+                    arrived(out_b, q)
+                    send_on(out_b, slot, q, here + gin[out_b, q].astype(F32), vin[out_b, q], onward)
+
+            @pl.when(coming & jnp.logical_not(in_text) & (in_b == chip) & (in_p % TALL == TALL - 1))
             def _():
-                arrived(home, in_p)
-                gt_ref[part_of(in_p), :] += gin[home, in_p].astype(F32) + vin[home, in_p]
+                q = in_p // TALL
+                arrived(home, q)
+                gt_ref[tall_part_of(q), :] += gin[home, q].astype(F32) + vin[home, q]
 
         @pl.when(s == window_at)
         def _():
@@ -245,18 +254,22 @@
                 def _():
                     all_text(b, b)
 
-    @pl.loop(0, n)
-    def _(b):
-        @pl.when(b != chip)
-        def _():
-            remote(gout.at[b], gout.at[b], g_send.at[b], g_recv.at[b, 0], partner).wait_send()
-            remote(vout.at[b], vout.at[b], v_send.at[b], v_recv.at[b, 0], partner).wait_send()
+                @pl.when((b > chip + 1) | (b < chip - 1))
+                def _():
+                    all_sums(b)
+
+    for side, (_, more, _, _, _) in enumerate(sides):
+        @pl.when(more)
+        def _():
+            all_sums(chip + 1 - 2 * side)
 
 
 def write_out(gi_ref, gt_ref, gi_out, gt_out, sem):
+    part = gi_ref.shape[0] // WRITES
     copies = [
-        pltpu.make_async_copy(gi_ref, gi_out, sem.at[0]),
-        pltpu.make_async_copy(gt_ref, gt_out, sem.at[1]),
+        pltpu.make_async_copy(src.at[pl.ds(w * part, part)], dst.at[pl.ds(w * part, part)], sem.at[m, w])
+        for w in range(WRITES)
+        for m, (src, dst) in enumerate(((gi_ref, gi_out), (gt_ref, gt_out)))
     ]
     for copy in copies:
         copy.start()
@@ -270,7 +283,7 @@
 
     def shards(images, texts, sharpness, offset):
         rows, width = images.shape
-        piece = rows // PIECES
+        tall, count = TALL * rows // PIECES, PIECES // TALL
         bf16 = jnp.bfloat16
         out = jax.ShapeDtypeStruct((rows, width), F32)
         vmem = pl.BlockSpec(memory_space=pltpu.VMEM)
@@ -291,16 +304,16 @@
                 pltpu.VMEM((rows, width), bf16),
                 pltpu.VMEM((n, rows, width), bf16),
                 pltpu.VMEM((n, 2, rows, rows), bf16),
-                pltpu.VMEM((n + 1, PIECES, piece, width), bf16),
-                pltpu.VMEM((n, PIECES, piece, width), bf16),
-                pltpu.VMEM((n + 1, PIECES, 1, width), F32),
-                pltpu.VMEM((n, PIECES, 1, width), F32),
+                pltpu.VMEM((n + 1, count, tall, width), bf16),
+                pltpu.VMEM((n, count, tall, width), bf16),
+                pltpu.VMEM((n + 1, count, 1, width), F32),
+                pltpu.VMEM((n, count, 1, width), F32),
                 dma((n + 1,)),
                 dma((n, PIECES)),
                 dma((n,)),
-                dma((n + 1, PIECES)),
+                dma((n + 1, count)),
                 dma((n,)),
-                dma((n + 1, PIECES)),
+                dma((n + 1, count)),
                 dma((4,)),
                 dma((4,)),
                 dma((2,)),
@@ -314,7 +327,7 @@
             out_shape=(out, out),
             in_specs=[vmem, vmem],
             out_specs=(hbm, hbm),
-            scratch_shapes=[dma((2,))],
+            scratch_shapes=[dma((2, WRITES))],
             compiler_params=pltpu.CompilerParams(vmem_limit_bytes=8 * 1024 * 1024),
         )(gi, gt)
 

time: 63 us -> 63 us (level)
  no operation moved by 1% of the time
where the time goes in v3:
time: 63 us; the launch traced here: 62.9 us
  Pallas kernels  60.9 us (97%)
  between operations  1.93 us (3%)
    pallas_call x1, Pallas kernels, shards(): pl.pallas_call(functools.partial(kernel, groups, n), out_shape=(out, out)...  59.5 us
    pallas_call x1, Pallas kernels, shards(): pl.pallas_call(write_out, out_shape=(out, out), in_specs=[vmem, vmem], ou...  1.47 us

profile of v3, /device:TPU:0, one launch (start us, length us, event | category | flops | bytes accessed | tf_op | source)
XLA Modules:
  0.0 62.9 jit_solution(4119829212513260343)
XLA Ops:
  1.9 59.5 %shard_map.59 = (f32[256,1152]{1,0:T(8,128)S(1)}, f32[256,1152]{1,0:T(8,128)S(1)}) custom-call(f32[1]{0:T(128)S(6)} %copy.6.sharp_ref, f32[1]{0:T(128)S(6)} %copy.7.bias_ref, bf16[256,1152]{1,0:T(8,128)(2,1)} %img_hbm.1, bf16[256,1152]{1,0:T(8,128)(2,1)} %txt_hbm.1), custom_call_target="tpu_custom_call" | custom-call | tf_op jit(solution)/shard_map/pallas_call | solution.py:293
  61.4 1.5 %shard_map.60 = (f32[256,1152]{1,0:T(8,128)}, f32[256,1152]{1,0:T(8,128)}) custom-call(f32[256,1152]{1,0:T(8,128)S(1)} %get-tuple-element.4.gi_ref, f32[256,1152]{1,0:T(8,128)S(1)} %get-tuple-element.5.gt_ref), custom_call_target="tpu_custom_call" | custom-call | tf_op jit(solution)/shard_map/pallas_call | solution.py:325

commit v4 on v3

--- a/solution.py
+++ b/solution.py
@@ -163,7 +163,7 @@
         remote(vout.at[b], vout.at[b], v_send.at[b], v_recv.at[b, 0], partner).wait_send()
 
     total_pieces = n * PIECES
-    window_at = (n - 1) * PIECES - 1
+    window_at = (n - 1) * PIECES - 8
     give_at = (n - 1) * PIECES + LAG
     take_at = total_pieces - 2
 
@@ -224,6 +224,9 @@
             to_ahead.wait_recv()
             c = weights(contract(img_ref[...], txt_prev[...], 1, 1), False)
             gi_ref[...] += contract(c, txt_prev[...], 1, 0)
+
+        @pl.when(s == window_at + 5)
+        def _():
             to_behind.wait_recv()
             c = weights(contract(own[...], img_next[...], 1, 1), False)
             gt_ref[...] += contract(c, img_next[...], 1, 0)

time: 63 us -> 63.1 us (level)
  no operation moved by 1% of the time
where the time goes in v4:
time: 63.1 us; the launch traced here: 62.9 us
  Pallas kernels  60.9 us (97%)
  between operations  1.93 us (3%)
    pallas_call x1, Pallas kernels, shards(): pl.pallas_call(functools.partial(kernel, groups, n), out_shape=(out, out)...  59.5 us
    pallas_call x1, Pallas kernels, shards(): pl.pallas_call(write_out, out_shape=(out, out), in_specs=[vmem, vmem], ou...  1.47 us

profile of v4, /device:TPU:0, one launch (start us, length us, event | category | flops | bytes accessed | tf_op | source)
XLA Modules:
  0.0 62.9 jit_solution(3533117542769375696)
XLA Ops:
  1.9 59.5 %shard_map.59 = (f32[256,1152]{1,0:T(8,128)S(1)}, f32[256,1152]{1,0:T(8,128)S(1)}) custom-call(f32[1]{0:T(128)S(6)} %copy.6.sharp_ref, f32[1]{0:T(128)S(6)} %copy.7.bias_ref, bf16[256,1152]{1,0:T(8,128)(2,1)} %img_hbm.1, bf16[256,1152]{1,0:T(8,128)(2,1)} %txt_hbm.1), custom_call_target="tpu_custom_call" | custom-call | tf_op jit(solution)/shard_map/pallas_call | solution.py:296
  61.4 1.5 %shard_map.60 = (f32[256,1152]{1,0:T(8,128)}, f32[256,1152]{1,0:T(8,128)}) custom-call(f32[256,1152]{1,0:T(8,128)S(1)} %get-tuple-element.4.gi_ref, f32[256,1152]{1,0:T(8,128)S(1)} %get-tuple-element.5.gt_ref), custom_call_target="tpu_custom_call" | custom-call | tf_op jit(solution)/shard_map/pallas_call | solution.py:328

commit v5 on v4

--- a/solution.py
+++ b/solution.py
@@ -11,10 +11,11 @@
 F32 = jnp.float32
 PIECES = 8
 TALL = 1
-WRITES = 4
+WRITES = 1
 HOP = 4
 AHEAD = 2
 LAG = 1
+TAKE_LAG = 2
 
 
 def contract(a, b, da, db):
@@ -167,7 +168,7 @@
     give_at = (n - 1) * PIECES + LAG
     take_at = total_pieces - 2
 
-    @pl.loop(0, total_pieces + LAG)
+    @pl.loop(0, total_pieces + TAKE_LAG)
     def _(s):
         for side, (k, more, onward, own_slot, home) in enumerate(sides):
             i, j = s + AHEAD, s - LAG
@@ -175,7 +176,10 @@
             in_text, in_b, in_p = order(j, k - 1, n)
             out_b, in_b = seen(side, out_b), seen(side, in_b)
             going = more & (i < total_pieces)
-            coming = (k > 0) & (j >= 0)
+            coming = (k > 0) & (j >= 0) & (j < total_pieces)
+            own_j = s - TAKE_LAG
+            own_text, own_b, own_p = order(own_j, k - 1, n)
+            own_b = seen(side, own_b)
 
             @pl.when(going & out_text & (out_b == chip) & (i >= HOP))
             def _():
@@ -185,7 +189,7 @@
 
             @pl.when((going & out_text & (out_b != chip)) | (jnp.logical_not(more) & coming & in_text))
             def _():
-                text(b, b, p, onward).wait_recv()
+                text(b, b, p, partner).wait_recv()
 
                 @pl.when(more)
                 def _():
@@ -213,9 +217,9 @@
                     arrived(out_b, q)
                     send_on(out_b, slot, q, here + gin[out_b, q].astype(F32), vin[out_b, q], onward)
 
-            @pl.when(coming & jnp.logical_not(in_text) & (in_b == chip) & (in_p % TALL == TALL - 1))
+            @pl.when((k > 0) & (own_j >= 0) & jnp.logical_not(own_text) & (own_b == chip) & (own_p % TALL == TALL - 1))
             def _():
-                q = in_p // TALL
+                q = own_p // TALL
                 arrived(home, q)
                 gt_ref[tall_part_of(q), :] += gin[home, q].astype(F32) + vin[home, q]
 

time: 63.1 us -> 62.2 us (0.986)
  Pallas kernels: 60.9 us -> 60 us
    pallas_call x1, Pallas kernels: 59.5 us -> 58.6 us  [shards(): pl.pallas_call(functools.partial(kernel, groups, n), out_shape=(out, out)...]
where the time goes in v5:
time: 62.2 us; the launch traced here: 61.9 us
  Pallas kernels  60 us (96%)
  between operations  1.93 us (3%)
    pallas_call x1, Pallas kernels, shards(): pl.pallas_call(functools.partial(kernel, groups, n), out_shape=(out, out)...  58.6 us
    pallas_call x1, Pallas kernels, shards(): pl.pallas_call(write_out, out_shape=(out, out), in_specs=[vmem, vmem], ou...  1.42 us

profile of v5, /device:TPU:0, one launch (start us, length us, event | category | flops | bytes accessed | tf_op | source)
XLA Modules:
  0.0 61.9 jit_solution(1775596195999614447)
XLA Ops:
  1.9 58.6 %shard_map.59 = (f32[256,1152]{1,0:T(8,128)S(1)}, f32[256,1152]{1,0:T(8,128)S(1)}) custom-call(f32[1]{0:T(128)S(6)} %copy.6.sharp_ref, f32[1]{0:T(128)S(6)} %copy.7.bias_ref, bf16[256,1152]{1,0:T(8,128)(2,1)} %img_hbm.1, bf16[256,1152]{1,0:T(8,128)(2,1)} %txt_hbm.1), custom_call_target="tpu_custom_call" | custom-call | tf_op jit(solution)/shard_map/pallas_call | solution.py:300
  60.5 1.4 %shard_map.60 = (f32[256,1152]{1,0:T(8,128)}, f32[256,1152]{1,0:T(8,128)}) custom-call(f32[256,1152]{1,0:T(8,128)S(1)} %get-tuple-element.4.gi_ref, f32[256,1152]{1,0:T(8,128)S(1)} %get-tuple-element.5.gt_ref), custom_call_target="tpu_custom_call" | custom-call | tf_op jit(solution)/shard_map/pallas_call | solution.py:332

commit v6 on v5

--- a/solution.py
+++ b/solution.py
@@ -10,12 +10,12 @@
 MESH = pl.DeviceIdType.MESH
 F32 = jnp.float32
 PIECES = 8
-TALL = 1
+TALL = 2
 WRITES = 1
 HOP = 4
 AHEAD = 2
 LAG = 1
-TAKE_LAG = 2
+TAKE_LAG = 3
 
 
 def contract(a, b, da, db):

time: 62.2 us -> 62.2 us (level)
  no operation moved by 1% of the time
where the time goes in v6:
time: 62.2 us; the launch traced here: 62 us
  Pallas kernels  60.1 us (97%)
  between operations  1.93 us (3%)
    pallas_call x1, Pallas kernels, shards(): pl.pallas_call(functools.partial(kernel, groups, n), out_shape=(out, out)...  58.7 us
    pallas_call x1, Pallas kernels, shards(): pl.pallas_call(write_out, out_shape=(out, out), in_specs=[vmem, vmem], ou...  1.42 us

profile of v6, /device:TPU:0, one launch (start us, length us, event | category | flops | bytes accessed | tf_op | source)
XLA Modules:
  0.0 62.0 jit_solution(15294289658799825606)
XLA Ops:
  1.9 58.7 %shard_map.59 = (f32[256,1152]{1,0:T(8,128)S(1)}, f32[256,1152]{1,0:T(8,128)S(1)}) custom-call(f32[1]{0:T(128)S(6)} %copy.6.sharp_ref, f32[1]{0:T(128)S(6)} %copy.7.bias_ref, bf16[256,1152]{1,0:T(8,128)(2,1)} %img_hbm.1, bf16[256,1152]{1,0:T(8,128)(2,1)} %txt_hbm.1), custom_call_target="tpu_custom_call" | custom-call | tf_op jit(solution)/shard_map/pallas_call | solution.py:300
  60.6 1.4 %shard_map.60 = (f32[256,1152]{1,0:T(8,128)}, f32[256,1152]{1,0:T(8,128)}) custom-call(f32[256,1152]{1,0:T(8,128)S(1)} %get-tuple-element.4.gi_ref, f32[256,1152]{1,0:T(8,128)S(1)} %get-tuple-element.5.gt_ref), custom_call_target="tpu_custom_call" | custom-call | tf_op jit(solution)/shard_map/pallas_call | solution.py:332
